TPU v7x, 128 devices: a whole 4x4x4 slice. The times are simulated.
128 devices in a mesh: tm: 8 (over z, core), space: 16 (over y, x).
Axes of the slice: x: 4, y: 4, z: 4, core: 2. Of those that a mesh axis runs over, the one named last changes fastest.
Arguments:
- noise: bfloat16 [32, 1024, 8192], P('tm', 'space'), may hold values from -4 to 4
- scale: float32 [32, 8192], P('tm'), may hold values from 0.55 to 1
- tiles: bfloat16 [32, 64, 3, 128, 128], P('tm', 'space'), may hold values from -0.375 to 0.375
- columns: int32 [32, 64, 3], P('tm', 'space'), may hold values from 0 to 63, as said below
Outputs:
- samples: bfloat16 [32, 1024, 8192], P('tm', 'space')
Inputs may be any that keep to these rules, and one draw needn't show every extreme that they name: `columns`: in every tile row r of a time step the 3 entries are different, and the first is r itself.
All inputs are finite; a program needn't handle non-finite values.
Results may differ from a plain program's by a relative error of at most 0.03.
Values may be sent and summed in bfloat16 or wider, within the bound.
No kernel may reach another device: no remote copies, remote signals or barrier semaphores. Data moves between devices by JAX's collectives and lax.ppermute only.
A program may use at most 128 MiB of HBM per device.

v0:
```python
import jax
import jax.numpy as jnp
from jax import lax
from jax.sharding import PartitionSpec as P


def shifted(shard, axis, by):
    devices = lax.axis_size(axis)
    pairs = [(i, i + by) for i in range(devices) if 0 <= i + by < devices]
    return lax.ppermute(shard, axis, pairs)


def on_device(noise, scale, tiles, columns):
    step_count = noise.shape[0]
    local_samples = noise.shape[1]
    node_count = noise.shape[2]
    tile_count = tiles.shape[2]
    tile_size = tiles.shape[3]
    tile_rows = node_count // tile_size
    part_count = lax.axis_size("tm")
    my_part = lax.axis_index("tm")
    block_count = 1
    block_width = local_samples // block_count
    tiles_by_k = jnp.transpose(tiles, (0, 2, 1, 3, 4))
    columns_by_k = jnp.transpose(columns, (0, 2, 1))
    noise_rows = noise.reshape(step_count, local_samples, tile_rows, tile_size).transpose(
        0, 2, 1, 3
    )
    scale_rows = scale.reshape(step_count, tile_rows, 1, tile_size)
    full_tiles, full_columns = (
        lax.all_gather(tiles_by_k, "space", axis=2, tiled=True),
        lax.all_gather(columns_by_k, "space", axis=2, tiled=True),
    )

    def step_operands(time_step):
        return (full_tiles[time_step], full_columns[time_step])

    def sweep(incoming):
        current = incoming
        produced = [None] * step_count
        for reverse_step in range(step_count):
            time_step = step_count - 1 - reverse_step
            step_tile, step_column = step_operands(time_step)
            mixed = jnp.zeros((tile_rows, block_width, tile_size), jnp.float32)
            for which in range(tile_count):
                picked = jnp.take(current, step_column[which], axis=0)
                mixed = mixed + jnp.einsum(
                    "rsj,rij->rsi", picked, step_tile[which], preferred_element_type=jnp.float32
                )
            noise_block = noise_rows[time_step]
            updated = scale_rows[time_step] * (noise_block.astype(jnp.float32) + mixed)
            current = updated.astype(jnp.bfloat16)
            produced[time_step] = current
        return (current, jnp.stack(produced))

    def section(section_index, loop_carry):
        front, result = loop_carry
        incoming = shifted(front, "tm", -1)
        block_index = section_index - (part_count - 1 - my_part)
        active = (block_index >= 0) & (block_index < block_count)
        row_start = jnp.clip(block_index, 0, block_count - 1) * block_width
        first_field, block_out = sweep(incoming)
        chosen = jnp.where(active, block_out, result)
        new_result = lax.dynamic_update_slice_in_dim(result, chosen, row_start, 2)
        new_front = jnp.where(active, first_field, front)
        return (new_front, new_result)

    start_front = jnp.zeros((tile_rows, block_width, tile_size), jnp.bfloat16)
    start_result = jnp.zeros((step_count, tile_rows, local_samples, tile_size), jnp.bfloat16)
    _, result = lax.fori_loop(0, part_count + block_count - 1, section, (start_front, start_result))
    return result.transpose(0, 2, 1, 3).reshape(step_count, local_samples, node_count)


def solution(mesh):
    placed = (
        P("tm", "space", None),
        P("tm", None),
        P("tm", "space", None, None, None),
        P("tm", "space", None),
    )
    return jax.shard_map(
        on_device, mesh=mesh, in_specs=placed, out_specs=P("tm", "space", None), check_vma=False
    )
```

profile of v0, /device:TPU:1, one launch (start us, length us, event | category | flops | bytes accessed | tf_op | source)
XLA Modules:
  0.0 834.2 jit_solution(8011077418723320846)
XLA Ops:
  13.7 4.7 copy.14
  18.6 21.3 %all_gather.6 = s32[4,3,64]{1,0,2:T(4,128)S(1)} all-gather(s32[4,3,4]{1,0,2:T(4,128)S(1)} %bitcast.179), channel_id=1, replica_groups=mesh['tm'=8,'space'=16] {'space'}, dimensions={2}, use_global_device_ids=true | all-gather | bytes 3264 | tf_op jit(solution)/shard_map/all_gather | solution.py:32
  40.0 127.4 %all-gather.2.cloned.1.call-done = bf16[4,3,64,128,128]{4,3,2,1,0:T(8,128)(2,1)} async-done(((bf16[4,3,4,128,128]{4,3,2,1,0:T(8,128)(2,1)}), bf16[4,3,64,128,128]{4,3,2,1,0:T(8,128)(2,1)}) %all-gather.2.cloned.1.call-update) | async-done | bytes 25165840 | tf_op jit(solution)/shard_map/all_gather | solution.py:31
  167.4 655.0 %while.18 = (s32[]{:T(128)}, bf16[64,64,128]{2,1,0:T(8,128)(2,1)}, bf16[4,64,64,128]{3,2,1,0:T(8,128)(2,1)}, s32[]{:T(128)}, f32[4,64,1,128]{3,1,2,0:T(8,128)S(1...) while((s32[]{:T(128)}, bf16[64,64,128]{2,1,0:T(8,128)(2,1)}, ...), condition=%wide.region_1.0_spmd.clone, body=%wide.region_0.2_spmd.clone.sunk | while | flops 1641038336 | bytes 185005984 | solution.py:70
  170.2 13.5 %collective-permute-done = bf16[64,64,128]{2,1,0:T(8,128)(2,1)S(1)} collective-permute-done((bf16[64,64,128]{2,1,0:T(8,128)(2,1)S(1)}, bf16[64,64,128]{2,1,0:T(8,128)(2,1)S(1)}, u32[]{:S(2)}, u32[]{:S(2)}) %collective-permute-start) | collective-permute-done | bytes 1048608 | tf_op jit(solution)/shard_map/while/body/eval_jaxpr/ppermute | solution.py:10
  190.6 4.8 fusion.158
  240.5 4.6 broadcast_select_fusion.5
  251.7 14.0 %collective-permute-done = bf16[64,64,128]{2,1,0:T(8,128)(2,1)S(1)} collective-permute-done((bf16[64,64,128]{2,1,0:T(8,128)(2,1)S(1)}, bf16[64,64,128]{2,1,0:T(8,128)(2,1)S(1)}, u32[]{:S(2)}, u32[]{:S(2)}) %collective-permute-start) | collective-permute-done | bytes 1048608 | tf_op jit(solution)/shard_map/while/body/eval_jaxpr/ppermute | solution.py:10
  272.6 4.8 fusion.158
  279.0 4.3 fusion.160
  322.6 4.6 broadcast_select_fusion.5
  333.7 14.0 %collective-permute-done = bf16[64,64,128]{2,1,0:T(8,128)(2,1)S(1)} collective-permute-done((bf16[64,64,128]{2,1,0:T(8,128)(2,1)S(1)}, bf16[64,64,128]{2,1,0:T(8,128)(2,1)S(1)}, u32[]{:S(2)}, u32[]{:S(2)}) %collective-permute-start) | collective-permute-done | bytes 1048608 | tf_op jit(solution)/shard_map/while/body/eval_jaxpr/ppermute | solution.py:10
  354.6 4.8 fusion.158
  361.1 4.3 fusion.160
  404.6 4.6 broadcast_select_fusion.5
  415.7 14.0 %collective-permute-done = bf16[64,64,128]{2,1,0:T(8,128)(2,1)S(1)} collective-permute-done((bf16[64,64,128]{2,1,0:T(8,128)(2,1)S(1)}, bf16[64,64,128]{2,1,0:T(8,128)(2,1)S(1)}, u32[]{:S(2)}, u32[]{:S(2)}) %collective-permute-start) | collective-permute-done | bytes 1048608 | tf_op jit(solution)/shard_map/while/body/eval_jaxpr/ppermute | solution.py:10
  436.6 4.8 fusion.158
  486.6 4.6 broadcast_select_fusion.5
  497.8 14.0 %collective-permute-done = bf16[64,64,128]{2,1,0:T(8,128)(2,1)S(1)} collective-permute-done((bf16[64,64,128]{2,1,0:T(8,128)(2,1)S(1)}, bf16[64,64,128]{2,1,0:T(8,128)(2,1)S(1)}, u32[]{:S(2)}, u32[]{:S(2)}) %collective-permute-start) | collective-permute-done | bytes 1048608 | tf_op jit(solution)/shard_map/while/body/eval_jaxpr/ppermute | solution.py:10
  518.7 4.8 fusion.158
  525.1 4.3 fusion.160
  568.6 4.6 broadcast_select_fusion.5
  579.8 14.0 %collective-permute-done = bf16[64,64,128]{2,1,0:T(8,128)(2,1)S(1)} collective-permute-done((bf16[64,64,128]{2,1,0:T(8,128)(2,1)S(1)}, bf16[64,64,128]{2,1,0:T(8,128)(2,1)S(1)}, u32[]{:S(2)}, u32[]{:S(2)}) %collective-permute-start) | collective-permute-done | bytes 1048608 | tf_op jit(solution)/shard_map/while/body/eval_jaxpr/ppermute | solution.py:10
  600.7 4.8 fusion.158
  650.6 4.6 broadcast_select_fusion.5
  661.8 14.0 %collective-permute-done = bf16[64,64,128]{2,1,0:T(8,128)(2,1)S(1)} collective-permute-done((bf16[64,64,128]{2,1,0:T(8,128)(2,1)S(1)}, bf16[64,64,128]{2,1,0:T(8,128)(2,1)S(1)}, u32[]{:S(2)}, u32[]{:S(2)}) %collective-permute-start) | collective-permute-done | bytes 1048608 | tf_op jit(solution)/shard_map/while/body/eval_jaxpr/ppermute | solution.py:10
  682.7 4.8 fusion.158
  732.7 4.6 broadcast_select_fusion.5
  743.8 14.0 %collective-permute-done = bf16[64,64,128]{2,1,0:T(8,128)(2,1)S(1)} collective-permute-done((bf16[64,64,128]{2,1,0:T(8,128)(2,1)S(1)}, bf16[64,64,128]{2,1,0:T(8,128)(2,1)S(1)}, u32[]{:S(2)}, u32[]{:S(2)}) %collective-permute-start) | collective-permute-done | bytes 1048608 | tf_op jit(solution)/shard_map/while/body/eval_jaxpr/ppermute | solution.py:10
  764.7 4.8 fusion.158
  814.7 4.6 broadcast_select_fusion.5
  822.5 4.9 copy_bitcast_fusion
  (403 shorter events, 460.2 us)
Async XLA Ops:
  6.5 160.9 %all-gather.2.cloned.1.call-start = ((), (), s32[]{:S(2)}) async-start(), calls=%async_computation | async-start | bytes 26738688 | tf_op jit(solution)/shard_map/all_gather | solution.py:31
  13.7 4.7 copy-start.9
  13.7 26.2 %copy-start.8 = (f32[4,8192]{1,0:T(4,128)S(1)}, f32[4,8192]{1,0:T(4,128)}, u32[]{:S(2)}) copy-start(f32[4,8192]{1,0:T(4,128)} %param.9) | copy-start | bytes 393220
  167.5 17.9 %copy-start.2 = (bf16[64,64,128]{2,1,0:T(8,128)(2,1)}, bf16[64,64,128]{2,1,0:T(8,128)(2,1)S(1)}, u32[]{:S(2)}) copy-start(bf16[64,64,128]{2,1,0:T(8,128)(2,1)S(1)} %broadcast_select_fusion.4) | copy-start | bytes 3145732 | tf_op jit(solution)/shard_map/while
  167.5 16.2 %collective-permute-start = (bf16[64,64,128]{2,1,0:T(8,128)(2,1)S(1)}, bf16[64,64,128]{2,1,0:T(8,128)(2,1)S(1)}, u32[]{:S(2)}, u32[]{:S(2)}) collective-permute-start(bf16[64,64,128]{2,1,0:T(8,128)(2,1)S(1)} %broadcast_select_fusion.4), channel_id=1, source_target_pairs={{16,0},{32,16},{48,32},{64,48},{80,64},{96,80},{112,96},{17,1},{33... | collective-permute-start | bytes 3145736 | tf_op jit(solution)/shard_map/while/body/eval_jaxpr/ppermute | solution.py:10
  240.5 4.6 copy-start
  249.6 17.8 %copy-start.2 = (bf16[64,64,128]{2,1,0:T(8,128)(2,1)}, bf16[64,64,128]{2,1,0:T(8,128)(2,1)S(1)}, u32[]{:S(2)}) copy-start(bf16[64,64,128]{2,1,0:T(8,128)(2,1)S(1)} %broadcast_select_fusion.4) | copy-start | bytes 3145732 | tf_op jit(solution)/shard_map/while
  249.6 16.1 %collective-permute-start = (bf16[64,64,128]{2,1,0:T(8,128)(2,1)S(1)}, bf16[64,64,128]{2,1,0:T(8,128)(2,1)S(1)}, u32[]{:S(2)}, u32[]{:S(2)}) collective-permute-start(bf16[64,64,128]{2,1,0:T(8,128)(2,1)S(1)} %broadcast_select_fusion.4), channel_id=1, source_target_pairs={{16,0},{32,16},{48,32},{64,48},{80,64},{96,80},{112,96},{17,1},{33... | collective-permute-start | bytes 3145736 | tf_op jit(solution)/shard_map/while/body/eval_jaxpr/ppermute | solution.py:10
  315.7 3.5 copy-start.7
  322.5 4.6 copy-start
  331.6 17.8 %copy-start.2 = (bf16[64,64,128]{2,1,0:T(8,128)(2,1)}, bf16[64,64,128]{2,1,0:T(8,128)(2,1)S(1)}, u32[]{:S(2)}) copy-start(bf16[64,64,128]{2,1,0:T(8,128)(2,1)S(1)} %broadcast_select_fusion.4) | copy-start | bytes 3145732 | tf_op jit(solution)/shard_map/while
  331.6 16.1 %collective-permute-start = (bf16[64,64,128]{2,1,0:T(8,128)(2,1)S(1)}, bf16[64,64,128]{2,1,0:T(8,128)(2,1)S(1)}, u32[]{:S(2)}, u32[]{:S(2)}) collective-permute-start(bf16[64,64,128]{2,1,0:T(8,128)(2,1)S(1)} %broadcast_select_fusion.4), channel_id=1, source_target_pairs={{16,0},{32,16},{48,32},{64,48},{80,64},{96,80},{112,96},{17,1},{33... | collective-permute-start | bytes 3145736 | tf_op jit(solution)/shard_map/while/body/eval_jaxpr/ppermute | solution.py:10
  397.7 3.5 copy-start.7
  404.6 4.6 copy-start
  413.6 17.8 %copy-start.2 = (bf16[64,64,128]{2,1,0:T(8,128)(2,1)}, bf16[64,64,128]{2,1,0:T(8,128)(2,1)S(1)}, u32[]{:S(2)}) copy-start(bf16[64,64,128]{2,1,0:T(8,128)(2,1)S(1)} %broadcast_select_fusion.4) | copy-start | bytes 3145732 | tf_op jit(solution)/shard_map/while
  413.7 16.1 %collective-permute-start = (bf16[64,64,128]{2,1,0:T(8,128)(2,1)S(1)}, bf16[64,64,128]{2,1,0:T(8,128)(2,1)S(1)}, u32[]{:S(2)}, u32[]{:S(2)}) collective-permute-start(bf16[64,64,128]{2,1,0:T(8,128)(2,1)S(1)} %broadcast_select_fusion.4), channel_id=1, source_target_pairs={{16,0},{32,16},{48,32},{64,48},{80,64},{96,80},{112,96},{17,1},{33... | collective-permute-start | bytes 3145736 | tf_op jit(solution)/shard_map/while/body/eval_jaxpr/ppermute | solution.py:10
  479.7 3.5 copy-start.7
  486.6 4.6 copy-start
  495.7 17.8 %copy-start.2 = (bf16[64,64,128]{2,1,0:T(8,128)(2,1)}, bf16[64,64,128]{2,1,0:T(8,128)(2,1)S(1)}, u32[]{:S(2)}) copy-start(bf16[64,64,128]{2,1,0:T(8,128)(2,1)S(1)} %broadcast_select_fusion.4) | copy-start | bytes 3145732 | tf_op jit(solution)/shard_map/while
  495.7 16.1 %collective-permute-start = (bf16[64,64,128]{2,1,0:T(8,128)(2,1)S(1)}, bf16[64,64,128]{2,1,0:T(8,128)(2,1)S(1)}, u32[]{:S(2)}, u32[]{:S(2)}) collective-permute-start(bf16[64,64,128]{2,1,0:T(8,128)(2,1)S(1)} %broadcast_select_fusion.4), channel_id=1, source_target_pairs={{16,0},{32,16},{48,32},{64,48},{80,64},{96,80},{112,96},{17,1},{33... | collective-permute-start | bytes 3145736 | tf_op jit(solution)/shard_map/while/body/eval_jaxpr/ppermute | solution.py:10
  568.6 4.6 copy-start
  577.7 17.8 %copy-start.2 = (bf16[64,64,128]{2,1,0:T(8,128)(2,1)}, bf16[64,64,128]{2,1,0:T(8,128)(2,1)S(1)}, u32[]{:S(2)}) copy-start(bf16[64,64,128]{2,1,0:T(8,128)(2,1)S(1)} %broadcast_select_fusion.4) | copy-start | bytes 3145732 | tf_op jit(solution)/shard_map/while
  577.7 16.1 %collective-permute-start = (bf16[64,64,128]{2,1,0:T(8,128)(2,1)S(1)}, bf16[64,64,128]{2,1,0:T(8,128)(2,1)S(1)}, u32[]{:S(2)}, u32[]{:S(2)}) collective-permute-start(bf16[64,64,128]{2,1,0:T(8,128)(2,1)S(1)} %broadcast_select_fusion.4), channel_id=1, source_target_pairs={{16,0},{32,16},{48,32},{64,48},{80,64},{96,80},{112,96},{17,1},{33... | collective-permute-start | bytes 3145736 | tf_op jit(solution)/shard_map/while/body/eval_jaxpr/ppermute | solution.py:10
  643.8 3.5 copy-start.7
  650.6 4.6 copy-start
  659.7 17.8 %copy-start.2 = (bf16[64,64,128]{2,1,0:T(8,128)(2,1)}, bf16[64,64,128]{2,1,0:T(8,128)(2,1)S(1)}, u32[]{:S(2)}) copy-start(bf16[64,64,128]{2,1,0:T(8,128)(2,1)S(1)} %broadcast_select_fusion.4) | copy-start | bytes 3145732 | tf_op jit(solution)/shard_map/while
  659.7 16.1 %collective-permute-start = (bf16[64,64,128]{2,1,0:T(8,128)(2,1)S(1)}, bf16[64,64,128]{2,1,0:T(8,128)(2,1)S(1)}, u32[]{:S(2)}, u32[]{:S(2)}) collective-permute-start(bf16[64,64,128]{2,1,0:T(8,128)(2,1)S(1)} %broadcast_select_fusion.4), channel_id=1, source_target_pairs={{16,0},{32,16},{48,32},{64,48},{80,64},{96,80},{112,96},{17,1},{33... | collective-permute-start | bytes 3145736 | tf_op jit(solution)/shard_map/while/body/eval_jaxpr/ppermute | solution.py:10
  725.8 3.5 copy-start.7
  732.6 4.6 copy-start
  741.7 17.8 %copy-start.2 = (bf16[64,64,128]{2,1,0:T(8,128)(2,1)}, bf16[64,64,128]{2,1,0:T(8,128)(2,1)S(1)}, u32[]{:S(2)}) copy-start(bf16[64,64,128]{2,1,0:T(8,128)(2,1)S(1)} %broadcast_select_fusion.4) | copy-start | bytes 3145732 | tf_op jit(solution)/shard_map/while
  741.7 16.1 %collective-permute-start = (bf16[64,64,128]{2,1,0:T(8,128)(2,1)S(1)}, bf16[64,64,128]{2,1,0:T(8,128)(2,1)S(1)}, u32[]{:S(2)}, u32[]{:S(2)}) collective-permute-start(bf16[64,64,128]{2,1,0:T(8,128)(2,1)S(1)} %broadcast_select_fusion.4), channel_id=1, source_target_pairs={{16,0},{32,16},{48,32},{64,48},{80,64},{96,80},{112,96},{17,1},{33... | collective-permute-start | bytes 3145736 | tf_op jit(solution)/shard_map/while/body/eval_jaxpr/ppermute | solution.py:10
  814.7 4.6 copy-start
  (43 other events, 130.9 us)
Sparse Core Ops, SparseCore 0:
  9.5 157.8 all-gather.1
where the time goes:
time: 836 us; the launch traced here: 834 us
  matrix products  350 us (42%)
  waiting for transfers between devices  239 us (29%)
  local copies, waits for them, and re-layouts  173 us (21%)
  blocking collectives  21.3 us (3%)
  other arithmetic  18.9 us (2%)
  starting transfers between devices  16 us (2%)
  between operations  13.5 us (2%)
    dot_general x96, matrix products, sweep(): jnp.einsum('rsj,rij->rsi', picked, step_tile[which], preferred_element_ty...  350 us
    gather x96, local copies, waits for them, and re-layouts, sweep(): picked = jnp.take(current, step_column[which], axis=0)  140 us
    all_gather x1, waiting for transfers between devices, on_device(): lax.all_gather(tiles_by_k, 'space', axis=2, tiled=True)  127 us
    ppermute x8, waiting for transfers between devices, shifted(): return lax.ppermute(shard, axis, pairs)  112 us
    all_gather x1, blocking collectives, on_device(): lax.all_gather(columns_by_k, 'space', axis=2, tiled=True)  21.3 us
  transfers between devices with their start and end apart: 9, of which 9 were waited for; matrix products, arithmetic and copies ran while one was open for 1% of the time, Pallas kernels for 0%

commit v1 on v0

--- a/solution.py
+++ b/solution.py
@@ -28,7 +28,9 @@
     )
     scale_rows = scale.reshape(step_count, tile_rows, 1, tile_size)
     full_tiles, full_columns = (
-        lax.all_gather(tiles_by_k, "space", axis=2, tiled=True),
+        jnp.concatenate(
+            lax.all_to_all(jnp.stack([tiles_by_k] * lax.axis_size("space")), "space", 0, 0), axis=2
+        ),
         lax.all_gather(columns_by_k, "space", axis=2, tiled=True),
     )
 

time: 836 us -> 1090 us (1.30)
  blocking collectives: 21.3 us -> 375 us
  waiting for transfers between devices: 239 us -> 112 us
  local copies, waits for them, and re-layouts: 173 us -> 203 us
  between operations: 13.5 us -> 0.09 us
  starting transfers between devices: 16 us -> 28.7 us
    all_gather x1, blocking collectives: 21.3 us -> 375 us  [on_device(): lax.all_gather(columns_by_k, 'space', axis=2, tiled=True)]
    all_gather x1 -> x0, waiting for transfers between devices: 127 us -> none  [on_device(): lax.all_gather(tiles_by_k, 'space', axis=2, tiled=True)]
    all_to_all x0 -> x1, local copies, waits for them, and re-layouts: none -> 21.1 us  [on_device(): lax.all_to_all(jnp.stack([tiles_by_k] * lax.axis_size('space')), 'space',...]
  transfers between devices with their start and end apart: 9 -> 9, of which waited for: 9 -> 8; matrix products, arithmetic and copies ran while one was open for 1% -> 1% of each run, Pallas kernels for 0% -> 0%
where the time goes in v1:
time: 1090 us
  blocking collectives  375 us (34%)
  matrix products  351 us (32%)
  local copies, waits for them, and re-layouts  203 us (19%)
  waiting for transfers between devices  112 us (10%)
  starting transfers between devices  28.7 us (3%)
  other arithmetic  18.9 us (2%)
    all_gather x1, blocking collectives, on_device(): lax.all_gather(columns_by_k, 'space', axis=2, tiled=True)  375 us
    dot_general x96, matrix products, sweep(): jnp.einsum('rsj,rij->rsi', picked, step_tile[which], preferred_element_ty...  351 us
    gather x96, local copies, waits for them, and re-layouts, sweep(): picked = jnp.take(current, step_column[which], axis=0)  140 us
    ppermute x8, waiting for transfers between devices, shifted(): return lax.ppermute(shard, axis, pairs)  112 us
  transfers between devices with their start and end apart: 9, of which 8 were waited for; matrix products, arithmetic and copies ran while one was open for 1% of the time, Pallas kernels for 0%

profile of v1, /device:TPU:1, one launch (start us, length us, event | category | flops | bytes accessed | tf_op | source)
XLA Modules:
  0.0 1090.7 jit_solution(4680546593511911621)
XLA Ops:
  1.5 9.0 stack.64
  10.5 7.6 all-to-all-start
  22.6 4.7 copy.20
  27.4 374.8 %all_gather.3 = s32[4,3,64]{1,0,2:T(4,128)S(1)} all-gather(s32[4,3,4]{1,0,2:T(4,128)S(1)} %bitcast.181), channel_id=1, replica_groups=mesh['tm'=8,'space'=16] {'space'}, dimensions={2}, use_global_device_ids=true | all-gather | bytes 3264 | tf_op jit(solution)/shard_map/all_gather | solution.py:34
  402.3 21.1 %copy.19 = bf16[16,4,3,4,128,128]{5,4,3,0,2,1:T(8,128)(2,1)} copy(bf16[16,4,3,4,128,128]{5,4,3,2,1,0:T(8,128)(2,1)} %all-to-all-done) | data formatting | bytes 50331648 | tf_op jit(solution)/shard_map/all_to_all | solution.py:32
  423.4 662.5 %while.18 = (s32[]{:T(128)}, bf16[64,64,128]{2,1,0:T(8,128)(2,1)}, bf16[4,64,64,128]{3,2,1,0:T(8,128)(2,1)}, s32[]{:T(128)}, f32[4,64,1,128]{3,1,2,0:T(8,128)S(1...) while((s32[]{:T(128)}, bf16[64,64,128]{2,1,0:T(8,128)(2,1)}, ...), condition=%wide.region_1.0_spmd.clone, body=%wide.region_0.2_spmd.clone.sunk | while | flops 1641038336 | bytes 185005984 | solution.py:72
  423.5 7.6 collective-permute-start
  431.2 13.8 %collective-permute-done = bf16[64,64,128]{2,1,0:T(8,128)(2,1)S(1)} collective-permute-done((bf16[64,64,128]{2,1,0:T(8,128)(2,1)S(1)}, bf16[64,64,128]{2,1,0:T(8,128)(2,1)S(1)}, u32[]{:S(2)}, u32[]{:S(2)}) %collective-permute-start) | collective-permute-done | bytes 1048608 | tf_op jit(solution)/shard_map/while/body/eval_jaxpr/ppermute | solution.py:10
  451.9 4.8 fusion.158
  502.0 4.7 broadcast_select_fusion.5
  513.3 14.0 %collective-permute-done = bf16[64,64,128]{2,1,0:T(8,128)(2,1)S(1)} collective-permute-done((bf16[64,64,128]{2,1,0:T(8,128)(2,1)S(1)}, bf16[64,64,128]{2,1,0:T(8,128)(2,1)S(1)}, u32[]{:S(2)}, u32[]{:S(2)}) %collective-permute-start) | collective-permute-done | bytes 1048608 | tf_op jit(solution)/shard_map/while/body/eval_jaxpr/ppermute | solution.py:10
  534.2 4.8 fusion.158
  584.3 4.7 broadcast_select_fusion.5
  595.6 14.0 %collective-permute-done = bf16[64,64,128]{2,1,0:T(8,128)(2,1)S(1)} collective-permute-done((bf16[64,64,128]{2,1,0:T(8,128)(2,1)S(1)}, bf16[64,64,128]{2,1,0:T(8,128)(2,1)S(1)}, u32[]{:S(2)}, u32[]{:S(2)}) %collective-permute-start) | collective-permute-done | bytes 1048608 | tf_op jit(solution)/shard_map/while/body/eval_jaxpr/ppermute | solution.py:10
  616.5 4.8 fusion.158
  666.6 4.7 broadcast_select_fusion.5
  677.9 14.0 %collective-permute-done = bf16[64,64,128]{2,1,0:T(8,128)(2,1)S(1)} collective-permute-done((bf16[64,64,128]{2,1,0:T(8,128)(2,1)S(1)}, bf16[64,64,128]{2,1,0:T(8,128)(2,1)S(1)}, u32[]{:S(2)}, u32[]{:S(2)}) %collective-permute-start) | collective-permute-done | bytes 1048608 | tf_op jit(solution)/shard_map/while/body/eval_jaxpr/ppermute | solution.py:10
  698.8 4.8 fusion.158
  748.9 4.7 broadcast_select_fusion.5
  760.1 14.0 %collective-permute-done = bf16[64,64,128]{2,1,0:T(8,128)(2,1)S(1)} collective-permute-done((bf16[64,64,128]{2,1,0:T(8,128)(2,1)S(1)}, bf16[64,64,128]{2,1,0:T(8,128)(2,1)S(1)}, u32[]{:S(2)}, u32[]{:S(2)}) %collective-permute-start) | collective-permute-done | bytes 1048608 | tf_op jit(solution)/shard_map/while/body/eval_jaxpr/ppermute | solution.py:10
  781.1 4.8 fusion.158
  831.1 4.7 broadcast_select_fusion.5
  842.4 14.0 %collective-permute-done = bf16[64,64,128]{2,1,0:T(8,128)(2,1)S(1)} collective-permute-done((bf16[64,64,128]{2,1,0:T(8,128)(2,1)S(1)}, bf16[64,64,128]{2,1,0:T(8,128)(2,1)S(1)}, u32[]{:S(2)}, u32[]{:S(2)}) %collective-permute-start) | collective-permute-done | bytes 1048608 | tf_op jit(solution)/shard_map/while/body/eval_jaxpr/ppermute | solution.py:10
  863.3 4.8 fusion.158
  913.4 4.7 broadcast_select_fusion.5
  924.7 14.0 %collective-permute-done = bf16[64,64,128]{2,1,0:T(8,128)(2,1)S(1)} collective-permute-done((bf16[64,64,128]{2,1,0:T(8,128)(2,1)S(1)}, bf16[64,64,128]{2,1,0:T(8,128)(2,1)S(1)}, u32[]{:S(2)}, u32[]{:S(2)}) %collective-permute-start) | collective-permute-done | bytes 1048608 | tf_op jit(solution)/shard_map/while/body/eval_jaxpr/ppermute | solution.py:10
  945.6 4.8 fusion.158
  995.7 4.7 broadcast_select_fusion.5
  1007.0 14.0 %collective-permute-done = bf16[64,64,128]{2,1,0:T(8,128)(2,1)S(1)} collective-permute-done((bf16[64,64,128]{2,1,0:T(8,128)(2,1)S(1)}, bf16[64,64,128]{2,1,0:T(8,128)(2,1)S(1)}, u32[]{:S(2)}, u32[]{:S(2)}) %collective-permute-start) | collective-permute-done | bytes 1048608 | tf_op jit(solution)/shard_map/while/body/eval_jaxpr/ppermute | solution.py:10
  1027.9 4.8 fusion.158
  1078.0 4.7 broadcast_select_fusion.5
  1085.9 4.9 copy_bitcast_fusion
  (404 shorter events, 470.7 us)
Async XLA Ops:
  10.5 391.8 %all-to-all-start = ((bf16[16,4,3,4,128,128]{5,4,3,2,1,0:T(8,128)(2,1)}), bf16[16,4,3,4,128,128]{5,4,3,2,1,0:T(8,128)(2,1)}, u32[]{:S(2)}, u32[]{:S(2)}) async-start(bf16[16,4,3,4,128,128]{5,4,3,2,1,0:T(8,128)(2,1)} %stack.64), calls=%async_computation | async-start | bytes 50331648 | tf_op jit(solution)/shard_map/all_to_all | solution.py:32
  22.5 4.7 copy-start.9
  22.6 379.7 %copy-start.8 = (f32[4,8192]{1,0:T(4,128)S(1)}, f32[4,8192]{1,0:T(4,128)}, u32[]{:S(2)}) copy-start(f32[4,8192]{1,0:T(4,128)} %param.9) | copy-start | bytes 393220
  423.5 23.3 %copy-start.2 = (bf16[64,64,128]{2,1,0:T(8,128)(2,1)}, bf16[64,64,128]{2,1,0:T(8,128)(2,1)S(1)}, u32[]{:S(2)}) copy-start(bf16[64,64,128]{2,1,0:T(8,128)(2,1)S(1)} %broadcast_select_fusion.4) | copy-start | bytes 3145732 | tf_op jit(solution)/shard_map/while
  423.5 21.6 %collective-permute-start = (bf16[64,64,128]{2,1,0:T(8,128)(2,1)S(1)}, bf16[64,64,128]{2,1,0:T(8,128)(2,1)S(1)}, u32[]{:S(2)}, u32[]{:S(2)}) collective-permute-start(bf16[64,64,128]{2,1,0:T(8,128)(2,1)S(1)} %broadcast_select_fusion.4), channel_id=1, source_target_pairs={{16,0},{32,16},{48,32},{64,48},{80,64},{96,80},{112,96},{17,1},{33... | collective-permute-start | bytes 3145736 | tf_op jit(solution)/shard_map/while/body/eval_jaxpr/ppermute | solution.py:10
  495.1 3.5 copy-start.7
  502.0 4.7 copy-start
  511.2 17.9 %copy-start.2 = (bf16[64,64,128]{2,1,0:T(8,128)(2,1)}, bf16[64,64,128]{2,1,0:T(8,128)(2,1)S(1)}, u32[]{:S(2)}) copy-start(bf16[64,64,128]{2,1,0:T(8,128)(2,1)S(1)} %broadcast_select_fusion.4) | copy-start | bytes 3145732 | tf_op jit(solution)/shard_map/while
  511.2 16.1 %collective-permute-start = (bf16[64,64,128]{2,1,0:T(8,128)(2,1)S(1)}, bf16[64,64,128]{2,1,0:T(8,128)(2,1)S(1)}, u32[]{:S(2)}, u32[]{:S(2)}) collective-permute-start(bf16[64,64,128]{2,1,0:T(8,128)(2,1)S(1)} %broadcast_select_fusion.4), channel_id=1, source_target_pairs={{16,0},{32,16},{48,32},{64,48},{80,64},{96,80},{112,96},{17,1},{33... | collective-permute-start | bytes 3145736 | tf_op jit(solution)/shard_map/while/body/eval_jaxpr/ppermute | solution.py:10
  577.4 3.5 copy-start.7
  584.3 4.7 copy-start
  593.5 17.9 %copy-start.2 = (bf16[64,64,128]{2,1,0:T(8,128)(2,1)}, bf16[64,64,128]{2,1,0:T(8,128)(2,1)S(1)}, u32[]{:S(2)}) copy-start(bf16[64,64,128]{2,1,0:T(8,128)(2,1)S(1)} %broadcast_select_fusion.4) | copy-start | bytes 3145732 | tf_op jit(solution)/shard_map/while
  593.5 16.1 %collective-permute-start = (bf16[64,64,128]{2,1,0:T(8,128)(2,1)S(1)}, bf16[64,64,128]{2,1,0:T(8,128)(2,1)S(1)}, u32[]{:S(2)}, u32[]{:S(2)}) collective-permute-start(bf16[64,64,128]{2,1,0:T(8,128)(2,1)S(1)} %broadcast_select_fusion.4), channel_id=1, source_target_pairs={{16,0},{32,16},{48,32},{64,48},{80,64},{96,80},{112,96},{17,1},{33... | collective-permute-start | bytes 3145736 | tf_op jit(solution)/shard_map/while/body/eval_jaxpr/ppermute | solution.py:10
  659.7 3.5 copy-start.7
  666.6 4.7 copy-start
  675.8 17.9 %copy-start.2 = (bf16[64,64,128]{2,1,0:T(8,128)(2,1)}, bf16[64,64,128]{2,1,0:T(8,128)(2,1)S(1)}, u32[]{:S(2)}) copy-start(bf16[64,64,128]{2,1,0:T(8,128)(2,1)S(1)} %broadcast_select_fusion.4) | copy-start | bytes 3145732 | tf_op jit(solution)/shard_map/while
  675.8 16.1 %collective-permute-start = (bf16[64,64,128]{2,1,0:T(8,128)(2,1)S(1)}, bf16[64,64,128]{2,1,0:T(8,128)(2,1)S(1)}, u32[]{:S(2)}, u32[]{:S(2)}) collective-permute-start(bf16[64,64,128]{2,1,0:T(8,128)(2,1)S(1)} %broadcast_select_fusion.4), channel_id=1, source_target_pairs={{16,0},{32,16},{48,32},{64,48},{80,64},{96,80},{112,96},{17,1},{33... | collective-permute-start | bytes 3145736 | tf_op jit(solution)/shard_map/while/body/eval_jaxpr/ppermute | solution.py:10
  742.0 3.5 copy-start.7
  748.8 4.7 copy-start
  758.1 17.9 %copy-start.2 = (bf16[64,64,128]{2,1,0:T(8,128)(2,1)}, bf16[64,64,128]{2,1,0:T(8,128)(2,1)S(1)}, u32[]{:S(2)}) copy-start(bf16[64,64,128]{2,1,0:T(8,128)(2,1)S(1)} %broadcast_select_fusion.4) | copy-start | bytes 3145732 | tf_op jit(solution)/shard_map/while
  758.1 16.1 %collective-permute-start = (bf16[64,64,128]{2,1,0:T(8,128)(2,1)S(1)}, bf16[64,64,128]{2,1,0:T(8,128)(2,1)S(1)}, u32[]{:S(2)}, u32[]{:S(2)}) collective-permute-start(bf16[64,64,128]{2,1,0:T(8,128)(2,1)S(1)} %broadcast_select_fusion.4), channel_id=1, source_target_pairs={{16,0},{32,16},{48,32},{64,48},{80,64},{96,80},{112,96},{17,1},{33... | collective-permute-start | bytes 3145736 | tf_op jit(solution)/shard_map/while/body/eval_jaxpr/ppermute | solution.py:10
  831.1 4.7 copy-start
  840.3 17.9 %copy-start.2 = (bf16[64,64,128]{2,1,0:T(8,128)(2,1)}, bf16[64,64,128]{2,1,0:T(8,128)(2,1)S(1)}, u32[]{:S(2)}) copy-start(bf16[64,64,128]{2,1,0:T(8,128)(2,1)S(1)} %broadcast_select_fusion.4) | copy-start | bytes 3145732 | tf_op jit(solution)/shard_map/while
  840.4 16.1 %collective-permute-start = (bf16[64,64,128]{2,1,0:T(8,128)(2,1)S(1)}, bf16[64,64,128]{2,1,0:T(8,128)(2,1)S(1)}, u32[]{:S(2)}, u32[]{:S(2)}) collective-permute-start(bf16[64,64,128]{2,1,0:T(8,128)(2,1)S(1)} %broadcast_select_fusion.4), channel_id=1, source_target_pairs={{16,0},{32,16},{48,32},{64,48},{80,64},{96,80},{112,96},{17,1},{33... | collective-permute-start | bytes 3145736 | tf_op jit(solution)/shard_map/while/body/eval_jaxpr/ppermute | solution.py:10
  913.4 4.7 copy-start
  922.6 17.9 %copy-start.2 = (bf16[64,64,128]{2,1,0:T(8,128)(2,1)}, bf16[64,64,128]{2,1,0:T(8,128)(2,1)S(1)}, u32[]{:S(2)}) copy-start(bf16[64,64,128]{2,1,0:T(8,128)(2,1)S(1)} %broadcast_select_fusion.4) | copy-start | bytes 3145732 | tf_op jit(solution)/shard_map/while
  922.6 16.1 %collective-permute-start = (bf16[64,64,128]{2,1,0:T(8,128)(2,1)S(1)}, bf16[64,64,128]{2,1,0:T(8,128)(2,1)S(1)}, u32[]{:S(2)}, u32[]{:S(2)}) collective-permute-start(bf16[64,64,128]{2,1,0:T(8,128)(2,1)S(1)} %broadcast_select_fusion.4), channel_id=1, source_target_pairs={{16,0},{32,16},{48,32},{64,48},{80,64},{96,80},{112,96},{17,1},{33... | collective-permute-start | bytes 3145736 | tf_op jit(solution)/shard_map/while/body/eval_jaxpr/ppermute | solution.py:10
  988.8 3.5 copy-start.7
  995.7 4.7 copy-start
  1004.9 17.9 %copy-start.2 = (bf16[64,64,128]{2,1,0:T(8,128)(2,1)}, bf16[64,64,128]{2,1,0:T(8,128)(2,1)S(1)}, u32[]{:S(2)}) copy-start(bf16[64,64,128]{2,1,0:T(8,128)(2,1)S(1)} %broadcast_select_fusion.4) | copy-start | bytes 3145732 | tf_op jit(solution)/shard_map/while
  1004.9 16.1 %collective-permute-start = (bf16[64,64,128]{2,1,0:T(8,128)(2,1)S(1)}, bf16[64,64,128]{2,1,0:T(8,128)(2,1)S(1)}, u32[]{:S(2)}, u32[]{:S(2)}) collective-permute-start(bf16[64,64,128]{2,1,0:T(8,128)(2,1)S(1)} %broadcast_select_fusion.4), channel_id=1, source_target_pairs={{16,0},{32,16},{48,32},{64,48},{80,64},{96,80},{112,96},{17,1},{33... | collective-permute-start | bytes 3145736 | tf_op jit(solution)/shard_map/while/body/eval_jaxpr/ppermute | solution.py:10
  1078.0 4.7 copy-start
  (43 other events, 131.6 us)
